TPU v7x, 128 devices: a whole 4x4x4 slice. The times are simulated.
128 devices in a mesh: row: 16 (over y, x), col: 4 (over z), dp: 2 (over core).
Axes of the slice: x: 4, y: 4, z: 4, core: 2. Of those that a mesh axis runs over, the one named last changes fastest.
Arguments:
- inputs: bfloat16 [1024, 8192], P(('col', 'dp'), 'row'), may hold values from -6 to 6
- gate_weight: bfloat16 [8192, 14336], P('row', 'col'), may hold values from -0.0625 to 0.0625
- up_weight: bfloat16 [8192, 14336], P('row', 'col'), may hold values from -0.0625 to 0.0625
- down_weight: bfloat16 [14336, 8192], P('col', 'row'), may hold values from -0.046875 to 0.046875
- reward_head: bfloat16 [8192], P('row'), may hold values from -0.0625 to 0.0625
- upstream: bfloat16 [1024, 8192], P(('col', 'dp'), 'row'), may hold values from -0.59765625 to 0.59765625
- labels: int32 [1024], P(('col', 'dp')), may hold values from 0 to 1
- label_mask: int32 [1024], P(('col', 'dp')), may hold values 0 or 1
Outputs:
- gate_grad: float32 [8192, 14336], P(('row', 'dp'), 'col')
- up_grad: float32 [8192, 14336], P(('row', 'dp'), 'col')
- down_grad: float32 [14336, 8192], P(('col', 'dp'), 'row')
- input_grad: float32 [1024, 8192], P(('col', 'dp'), 'row')
All inputs are finite; a program needn't handle non-finite values. No bound on the sum of `label_mask` on one device may be relied on, other than what follows from the above.
Results may differ from a plain program's by a relative error of at most 0.035.
Values may be sent and summed in bfloat16 or wider, within the bound.
No kernel may reach another device: no remote copies, remote signals or barrier semaphores. Data moves between devices by JAX's collectives and lax.ppermute only.
A program may use at most 128 MiB of HBM per device.

v0:
```python
import jax
import jax.numpy as jnp
from jax import lax
from jax.sharding import PartitionSpec as P

reward_weight = 8.0


def transpose_product(left, right):
    return lax.dot_general(
        left, right, (((0,), (0,)), ((), ())), preferred_element_type=jnp.float32
    )


def right_transpose(left, right):
    return lax.dot_general(
        left, right, (((1,), (1,)), ((), ())), preferred_element_type=jnp.float32
    )


def gather_tokens(block):
    return lax.all_gather(block, "col", axis=0, tiled=True)


def gather_hidden(stacked):
    return lax.all_gather(stacked, "row", axis=1, tiled=True)


def column_total(term_fn, count_rows):
    return lax.psum_scatter(
        term_fn(jnp.int32(0), count_rows * lax.axis_size("col")).astype(jnp.bfloat16),
        "col",
        scatter_dimension=0,
        tiled=True,
    ).astype(jnp.float32)


def per_device(
    inputs, gate_weight, up_weight, down_weight, reward_head, upstream, labels, label_mask
):
    width = gate_weight.shape[1]
    gathered = gather_tokens(inputs)
    rows = gathered
    joined = lax.psum_scatter(
        jnp.concatenate(
            [
                jnp.dot(rows, gate_weight, preferred_element_type=jnp.float32),
                jnp.dot(rows, up_weight, preferred_element_type=jnp.float32),
            ],
            axis=1,
        ).astype(jnp.bfloat16),
        "row",
        scatter_dimension=0,
        tiled=True,
    ).astype(jnp.float32)
    gate = joined[:, :width]
    upper = joined[:, width:]
    sigmoid_gate = jax.nn.sigmoid(gate)
    hidden = (gate * sigmoid_gate * upper).astype(jnp.bfloat16)
    hidden_all = gather_hidden(hidden[None])[0]

    def output_term(start, count):
        return jnp.dot(hidden_all, down_weight, preferred_element_type=jnp.float32)

    mixed = column_total(output_term, inputs.shape[0])
    outcome = inputs.astype(jnp.float32) + mixed
    head_value = reward_head.astype(jnp.float32)
    partial_score = jnp.dot(outcome, head_value, precision=lax.Precision.HIGHEST)
    score = lax.psum(partial_score, "row")
    slope = (
        reward_weight
        * label_mask.astype(jnp.float32)
        * (jax.nn.sigmoid(score) - labels.astype(jnp.float32))
    )
    grad_out = upstream.astype(jnp.float32) + slope[:, None] * head_value[None, :]
    grad_mixed = grad_out.astype(jnp.bfloat16)
    grad_rows = gather_tokens(grad_mixed)
    rows = grad_rows
    grad_hidden = lax.psum_scatter(
        right_transpose(rows, down_weight).astype(jnp.bfloat16),
        "row",
        scatter_dimension=0,
        tiled=True,
    ).astype(jnp.float32)
    grad_gate = (grad_hidden * upper * sigmoid_gate * (1.0 + gate * (1.0 - sigmoid_gate))).astype(
        jnp.bfloat16
    )
    grad_upper = (grad_hidden * gate * sigmoid_gate).astype(jnp.bfloat16)
    grads_all = gather_hidden(jnp.stack([grad_gate, grad_upper]))

    def input_term(start, count):
        return right_transpose(grads_all[0], gate_weight) + right_transpose(grads_all[1], up_weight)

    input_grad = grad_out + column_total(input_term, inputs.shape[0])
    gate_grad, up_grad, down_grad = (
        lax.psum_scatter(
            transpose_product(gathered, grads_all[0]).astype(jnp.bfloat16),
            "dp",
            scatter_dimension=0,
            tiled=True,
        ).astype(jnp.float32),
        lax.psum_scatter(
            transpose_product(gathered, grads_all[1]).astype(jnp.bfloat16),
            "dp",
            scatter_dimension=0,
            tiled=True,
        ).astype(jnp.float32),
        lax.psum_scatter(
            transpose_product(hidden_all, grad_rows).astype(jnp.bfloat16),
            "dp",
            scatter_dimension=0,
            tiled=True,
        ).astype(jnp.float32),
    )
    return (gate_grad, up_grad, down_grad, input_grad)


def solution(mesh):
    in_specs = (
        P(("col", "dp"), "row"),
        P("row", "col"),
        P("row", "col"),
        P("col", "row"),
        P("row"),
        P(("col", "dp"), "row"),
        P(("col", "dp")),
        P(("col", "dp")),
    )
    out_specs = (
        P(("row", "dp"), "col"),
        P(("row", "dp"), "col"),
        P(("col", "dp"), "row"),
        P(("col", "dp"), "row"),
    )
    return jax.shard_map(
        per_device, mesh=mesh, in_specs=in_specs, out_specs=out_specs, check_vma=False
    )
```

profile of v0, /device:TPU:1, one launch (start us, length us, event | category | flops | bytes accessed | tf_op | source)
XLA Modules:
  0.0 488.5 jit_solution(17730826505208931112)
XLA Ops:
  7.2 0.0 reduce-scatter.8.cloned.1.call-start
  7.2 13.6 %all_gather.12 = bf16[512,512]{1,0:T(8,128)(2,1)S(1)} all-gather(bf16[128,512]{1,0:T(8,128)(2,1)} %param.8), channel_id=1, replica_groups=mesh['row'=16,'col'=4,'dp'=2] {'col'}, dimensions={0}, use_global_device_ids=true | all-gather | bytes 655360 | tf_op jit(solution)/shard_map/all_gather | solution.py:22
  20.8 0.0 copy-start.6
  20.8 4.3 convolution_convert_fusion.4
  25.1 0.0 copy-done.6
  25.1 3.9 convolution_convert_fusion.5
  29.0 6.0 %pad_maximum_fusion = bf16[512,7168]{1,0:T(8,128)(2,1)} fusion(bf16[512,3584]{1,0:T(8,128)(2,1)S(1)} %convolution_convert_fusion.4, bf16[512,3584]{1,0:T(8,128)(2,1)} %convolution_convert_fusion.5), kind=kLoop, calls=%fused_computation | loop fusion | flops 14680064 | bytes 14680064 | tf_op jit(solution)/shard_map/concatenate | solution.py:45
  35.0 0.0 reduce-scatter.8.cloned.1.call-update
  35.0 0.0 all-gather.6.cloned.1.call-start
  35.1 84.9 %reduce-scatter.8.cloned.1.call-done = bf16[32,7168]{1,0:T(8,128)(2,1)} async-done(((bf16[512,7168]{1,0:T(8,128)(2,1)}), bf16[32,7168]{1,0:T(8,128)(2,1)}) %reduce-scatter.8.cloned.1.call-update) | async-done | bytes 458768 | tf_op jit(solution)/shard_map/reduce_scatter | solution.py:44
  120.0 1.1 convert_element_type.76
  121.1 0.8 multiply_convert_fusion
  121.9 0.0 all-gather.6.cloned.1.call-update
  121.9 0.0 copy-start.2
  121.9 0.0 copy-start
  122.0 0.0 copy-start.3
  122.0 0.0 copy-start.4
  122.0 0.0 copy-start.1
  122.0 0.0 reduce-scatter.10.cloned.1.call-start
  122.0 50.6 %all-gather.6.cloned.1.call-done = bf16[512,3584]{1,0:T(8,128)(2,1)} async-done(((bf16[32,3584]{1,0:T(8,128)(2,1)}), bf16[512,3584]{1,0:T(8,128)(2,1)}) %all-gather.6.cloned.1.call-update) | async-done | bytes 3670032 | tf_op jit(solution)/shard_map/all_gather | solution.py:26
  172.7 6.0 %convolution_convert_fusion.6 = bf16[512,512]{1,0:T(8,128)(2,1)} fusion(bf16[512,3584]{1,0:T(8,128)(2,1)} %all-gather.6.cloned.1.call-done, bf16[3584,512]{1,0:T(8,128)(2,1)} %param.11), kind=kOutput, calls=%fused_computation.15 | convolution fusion | flops 1879310336 | bytes 7864320 | tf_op jit(solution)/shard_map/dot_general | solution.py:63
  178.7 0.0 reduce-scatter.10.cloned.1.call-update
  178.7 0.0 reduce-scatter.12.cloned.1.call-start
  178.7 0.0 copy-done.2
  178.8 19.6 %reduce-scatter.10.cloned.1.call-done = bf16[128,512]{1,0:T(8,128)(2,1)} async-done(((bf16[512,512]{1,0:T(8,128)(2,1)}), bf16[128,512]{1,0:T(8,128)(2,1)}) %reduce-scatter.10.cloned.1.call-update) | async-done | bytes 131088 | tf_op jit(solution)/shard_map/reduce_scatter | solution.py:30
  198.4 0.0 copy-done
  198.4 1.1 convolution_bitcast_fusion
  199.5 33.2 %psum.7 = f32[128]{0:T(128)S(1)} all-reduce(f32[128]{0:T(128)S(1)} %convolution_bitcast_fusion), channel_id=1, replica_groups=mesh['row'=16,'col'=4,'dp'=2] {'row'}, use_global_device_ids=true, to_apply=%region_2.0 | all-reduce | flops 128 | bytes 1024 | tf_op jit(solution)/shard_map/psum | solution.py:69
  232.7 0.0 copy-done.3
  232.7 0.0 copy-done.4
  232.7 0.0 copy-done.1
  232.7 0.1 fusion.14
  232.8 10.2 %all_gather.14 = bf16[512,512]{1,0:T(8,128)(2,1)S(1)} all-gather(bf16[128,512]{1,0:T(8,128)(2,1)S(1)} %fusion.14), channel_id=1, replica_groups=mesh['row'=16,'col'=4,'dp'=2] {'col'}, dimensions={0}, use_global_device_ids=true | all-gather | bytes 655360 | tf_op jit(solution)/shard_map/all_gather | solution.py:22
  243.0 6.0 %convolution_convert_fusion.3 = bf16[512,3584]{1,0:T(8,128)(2,1)} fusion(bf16[512,512]{1,0:T(8,128)(2,1)S(1)} %all_gather.14, bf16[3584,512]{1,0:T(8,128)(2,1)} %param.11), kind=kOutput, calls=%fused_computation.4 | convolution fusion | flops 1880883200 | bytes 7864320 | tf_op jit(solution)/shard_map/dot_general | solution.py:16
  249.0 0.0 reduce-scatter.12.cloned.1.call-update
  249.0 0.0 all-gather.4.cloned.1.call-start
  249.1 81.0 %reduce-scatter.12.cloned.1.call-done = bf16[32,3584]{1,0:T(8,128)(2,1)} async-done(((bf16[512,3584]{1,0:T(8,128)(2,1)}), bf16[32,3584]{1,0:T(8,128)(2,1)}) %reduce-scatter.12.cloned.1.call-update) | async-done | bytes 229392 | tf_op jit(solution)/shard_map/reduce_scatter | solution.py:79
  330.0 1.2 fusion.16
  331.2 0.8 pad_maximum_fusion.1
  332.0 0.0 all-gather.4.cloned.1.call-update
  332.0 0.0 reduce-scatter.18.cloned.1.call-start
  332.1 6.0 %convolution_convert_fusion = bf16[3584,512]{1,0:T(8,128)(2,1)} fusion(bf16[512,3584]{1,0:T(8,128)(2,1)} %all-gather.6.cloned.1.call-done, bf16[512,512]{1,0:T(8,128)(2,1)S(1)} %all_gather.14), kind=kOutput, calls=%fused_computation.1 | convolution fusion | flops 1880883200 | bytes 7864320 | tf_op jit(solution)/shard_map/dot_general | solution.py:10
  338.0 0.0 reduce-scatter.18.cloned.1.call-update
  338.1 0.0 reduce-scatter.20.cloned.1.call-start
  338.1 61.8 %all-gather.4.cloned.1.call-done = bf16[2,512,3584]{2,1,0:T(8,128)(2,1)} async-done(((bf16[2,32,3584]{2,1,0:T(8,128)(2,1)}), bf16[2,512,3584]{2,1,0:T(8,128)(2,1)}) %all-gather.4.cloned.1.call-update) | async-done | bytes 7340048 | tf_op jit(solution)/shard_map/all_gather | solution.py:26
  399.9 5.4 %fusion.2 = f32[512,512]{1,0:T(8,128)S(1)} fusion(bf16[512,3584]{1,0:T(8,128)(2,1)} %param.9, bf16[2,512,3584]{2,1,0:T(8,128)(2,1)} %all-gather.4.cloned.1.call-done), kind=kOutput, calls=%fused_computation.11 | convolution fusion | flops 1879048192 | bytes 8388608 | tf_op jit(solution)/shard_map/dot_general | solution.py:16
  405.3 0.0 copy-done.5
  405.3 0.9 copy-done.7
  406.1 2.9 fusion.5
  409.0 0.0 reduce-scatter.20.cloned.1.call-update
  409.1 0.2 reduce-scatter.16.cloned.1.call-start
  409.3 6.0 %fusion.1 = bf16[512,3584]{0,1:T(8,128)(2,1)} fusion(bf16[512,512]{1,0:T(8,128)(2,1)S(1)} %all_gather.12, bf16[2,512,3584]{2,1,0:T(8,128)(2,1)} %all-gather.4.cloned.1.call-done), kind=kOutput, calls=%fused_computation.8 | convolution fusion | flops 1880883200 | bytes 7864320 | tf_op jit(solution)/shard_map/dot_general | solution.py:10
  415.3 0.0 reduce-scatter.16.cloned.1.call-update
  415.3 0.0 reduce-scatter.14.cloned.1.call-start
  415.4 6.3 %fusion = bf16[512,3584]{0,1:T(8,128)(2,1)} fusion(bf16[512,512]{1,0:T(8,128)(2,1)S(1)} %all_gather.12, bf16[2,512,3584]{2,1,0:T(8,128)(2,1)} %all-gather.4.cloned.1.call-done), kind=kOutput, calls=%fused_computation.7 | convolution fusion | flops 1880883200 | bytes 7864320 | tf_op jit(solution)/shard_map/dot_general | solution.py:10
  421.6 0.0 reduce-scatter.14.cloned.1.call-update
  421.6 0.0 reduce-scatter.18.cloned.1.call-done
  421.7 3.9 convert_element_type.94
  425.5 14.9 %reduce-scatter.20.cloned.1.call-done = bf16[128,512]{1,0:T(8,128)(2,1)} async-done(((bf16[512,512]{1,0:T(8,128)(2,1)}), bf16[128,512]{1,0:T(8,128)(2,1)}) %reduce-scatter.20.cloned.1.call-update) | async-done | bytes 131088 | tf_op jit(solution)/shard_map/reduce_scatter | solution.py:30
  440.5 1.7 convert_add_fusion
  442.2 17.1 %reduce-scatter.16.cloned.1.call-done = bf16[256,3584]{0,1:T(8,128)(2,1)} async-done(((bf16[512,3584]{0,1:T(8,128)(2,1)}), bf16[256,3584]{0,1:T(8,128)(2,1)}) %reduce-scatter.16.cloned.1.call-update) | async-done | bytes 1835024 | tf_op jit(solution)/shard_map/reduce_scatter | solution.py:102
  459.3 4.0 copy.13
  463.3 14.7 %reduce-scatter.14.cloned.1.call-done = bf16[256,3584]{0,1:T(8,128)(2,1)} async-done(((bf16[512,3584]{0,1:T(8,128)(2,1)}), bf16[256,3584]{0,1:T(8,128)(2,1)}) %reduce-scatter.14.cloned.1.call-update) | async-done | bytes 1835024 | tf_op jit(solution)/shard_map/reduce_scatter | solution.py:96
  478.0 4.0 copy.12
  (5 shorter events, 0.0 us)
Async XLA Ops:
  7.2 112.8 %reduce-scatter.8.cloned.1.call-start = ((), (), s32[]{:S(2)}) async-start(), calls=%async_computation.7 | async-start | bytes 7798784 | tf_op jit(solution)/shard_map/reduce_scatter | solution.py:44
  20.8 4.3 copy-start.6
  35.0 137.6 %all-gather.6.cloned.1.call-start = ((), (), s32[]{:S(2)}) async-start(), calls=%async_computation.15 | async-start | bytes 3899392 | tf_op jit(solution)/shard_map/all_gather | solution.py:26
  121.9 56.8 %copy-start.2 = (bf16[512]{0:T(512)(128)(2,1)S(1)}, bf16[512]{0:T(512)(128)(2,1)}, u32[]{:S(2)}) copy-start(bf16[512]{0:T(512)(128)(2,1)} %param.12) | copy-start | bytes 3076
  121.9 76.5 %copy-start = (bf16[128,512]{1,0:T(8,128)(2,1)S(1)}, bf16[128,512]{1,0:T(8,128)(2,1)}, u32[]{:S(2)}) copy-start(bf16[128,512]{1,0:T(8,128)(2,1)} %param.8) | copy-start | bytes 393220
  122.0 110.7 %copy-start.3 = (s32[128]{0:T(128)S(1)}, s32[128]{0:T(128)}, u32[]{:S(2)}) copy-start(s32[128]{0:T(128)} %param.14) | copy-start | bytes 1540
  122.0 110.7 %copy-start.4 = (s32[128]{0:T(128)S(1)}, s32[128]{0:T(128)}, u32[]{:S(2)}) copy-start(s32[128]{0:T(128)} %param.15) | copy-start | bytes 1540
  122.0 110.7 %copy-start.1 = (bf16[128,512]{1,0:T(8,128)(2,1)S(1)}, bf16[128,512]{1,0:T(8,128)(2,1)}, u32[]{:S(2)}) copy-start(bf16[128,512]{1,0:T(8,128)(2,1)} %param.13) | copy-start | bytes 393220
  122.0 76.4 %reduce-scatter.10.cloned.1.call-start = ((), (), s32[]{:S(2)}) async-start(), calls=%async_computation.8 | async-start | bytes 655360 | tf_op jit(solution)/shard_map/reduce_scatter | solution.py:30
  178.7 151.3 %reduce-scatter.12.cloned.1.call-start = ((), (), s32[]{:S(2)}) async-start(), calls=%async_computation.9 | async-start | bytes 3899392 | tf_op jit(solution)/shard_map/reduce_scatter | solution.py:79
  249.0 150.9 %all-gather.4.cloned.1.call-start = ((), (), s32[]{:S(2)}) async-start(), calls=%async_computation.10 | async-start | bytes 7798784 | tf_op jit(solution)/shard_map/all_gather | solution.py:26
  332.0 89.7 %reduce-scatter.18.cloned.1.call-start = ((), (), s32[]{:S(2)}) async-start(), calls=%async_computation.13 | async-start | bytes 5505024 | tf_op jit(solution)/shard_map/reduce_scatter | solution.py:108
  338.1 102.4 %reduce-scatter.20.cloned.1.call-start = ((), (), s32[]{:S(2)}) async-start(), calls=%async_computation.14 | async-start | bytes 655360 | tf_op jit(solution)/shard_map/reduce_scatter | solution.py:30
  399.9 5.4 %copy-start.5 = (bf16[2,512,3584]{2,1,0:T(8,128)(2,1)S(1)}, bf16[2,512,3584]{2,1,0:T(8,128)(2,1)}, u32[]{:S(2)}) copy-start(bf16[2,512,3584]{2,1,0:T(8,128)(2,1)} %all-gather.4.cloned.1.call-done) | copy-start | bytes 22020100
  399.9 6.3 %copy-start.7 = (bf16[512,3584]{1,0:T(8,128)(2,1)S(1)}, bf16[512,3584]{1,0:T(8,128)(2,1)}, u32[]{:S(2)}) copy-start(bf16[512,3584]{1,0:T(8,128)(2,1)} %param.10) | copy-start | bytes 11010052
  409.1 50.3 %reduce-scatter.16.cloned.1.call-start = ((), (), s32[]{:S(2)}) async-start(), calls=%async_computation.12 | async-start | bytes 5505024 | tf_op jit(solution)/shard_map/reduce_scatter | solution.py:102
  415.3 62.7 %reduce-scatter.14.cloned.1.call-start = ((), (), s32[]{:S(2)}) async-start(), calls=%async_computation.11 | async-start | bytes 5505024 | tf_op jit(solution)/shard_map/reduce_scatter | solution.py:96
Sparse Core Ops, SparseCore 0:
  35.1 84.8 reduce-scatter.7
  122.9 49.6 all-gather.5
  178.8 19.5 reduce-scatter.9
  249.1 80.8 reduce-scatter.11
  332.8 67.0 all-gather.3
  402.8 14.3 reduce-scatter.17
  419.6 20.8 reduce-scatter.19
  443.4 15.8 reduce-scatter.15
  462.4 15.5 reduce-scatter.13
where the time goes:
time: 489 us; the launch traced here: 488 us
  waiting for transfers between devices  345 us (71%)
  blocking collectives  56.9 us (12%)
  matrix products  47.8 us (10%)
  other arithmetic  15.5 us (3%)
  between operations  14 us (3%)
  local copies, waits for them, and re-layouts  8.87 us (2%)
    all_gather x2, waiting for transfers between devices, gather_hidden(): return lax.all_gather(stacked, 'row', axis=1, tiled=True)  112 us
    reduce_scatter x1, waiting for transfers between devices, per_device(): lax.psum_scatter(jnp.concatenate([jnp.dot(rows, gate_weight, preferred_el...  84.9 us
    reduce_scatter x1, waiting for transfers between devices, per_device(): lax.psum_scatter(right_transpose(rows, down_weight).astype(jnp.bfloat16),...  81 us
    reduce_scatter x2, waiting for transfers between devices, column_total(): lax.psum_scatter(term_fn(jnp.int32(0), count_rows * lax.axis_size('col'))...  34.6 us
    psum x1, blocking collectives, per_device(): score = lax.psum(partial_score, 'row')  33.2 us
    all_gather x2, blocking collectives, gather_tokens(): return lax.all_gather(block, 'col', axis=0, tiled=True)  23.8 us
    dot_general x3, matrix products, transpose_product(): lax.dot_general(left, right, (((0,), (0,)), ((), ())), preferred_element_...  18.2 us
    reduce_scatter x1, waiting for transfers between devices, per_device(): lax.psum_scatter(transpose_product(gathered, grads_all[1]).astype(jnp.bfl...  17.1 us
  transfers between devices with their start and end apart: 9, of which 8 were waited for; matrix products, arithmetic and copies ran while one was open for 7% of the time, Pallas kernels for 0%

commit v1 on v0

--- a/solution.py
+++ b/solution.py
@@ -4,6 +4,34 @@
 from jax.sharding import PartitionSpec as P
 
 reward_weight = 8.0
+
+
+def divide_the_slots(inner_x):
+    across = "row"
+    t_next = lax.axis_size(across)
+    reached = lax.axis_index(across)
+    a_next, w_next, passed = (t_next, reached, inner_x.shape[1])
+    vals = [idx * a_next if no == 1 else idx for no, idx in enumerate(inner_x.shape)]
+    formed = jnp.zeros(vals, inner_x.dtype)
+    val2 = lax.dynamic_update_slice_in_dim(formed, inner_x, w_next * passed, axis=1)
+    view_out = far_arr = inner_x
+    for j0 in range(1, a_next // 2 + 1):
+        last = range(a_next)
+        arr_out = map(lambda no: (no, (no + 1) % a_next), last)
+        view_out = lax.ppermute(view_out, axis_name=across, perm=list(arr_out))
+        val2 = lax.dynamic_update_slice_in_dim(
+            val2, view_out, (w_next - j0) % a_next * passed, axis=1
+        )
+        if 2 * j0 < a_next:
+            far_arr = lax.ppermute(
+                far_arr,
+                axis_name=across,
+                perm=list(map(lambda no: (no, (no - 1) % a_next), range(a_next))),
+            )
+            val2 = lax.dynamic_update_slice_in_dim(
+                val2, far_arr, (w_next + j0) % a_next * passed, axis=1
+            )
+    return val2
 
 
 def transpose_product(left, right):
@@ -23,7 +51,7 @@
 
 
 def gather_hidden(stacked):
-    return lax.all_gather(stacked, "row", axis=1, tiled=True)
+    return divide_the_slots(stacked)
 
 
 def column_total(term_fn, count_rows):

time: 489 us -> 545 us (1.11)
  starting transfers between devices: 0.55 us -> 71.1 us
  waiting for transfers between devices: 345 us -> 302 us
  local copies, waits for them, and re-layouts: 8.87 us -> 36.1 us
    all_gather x2 -> x0, waiting for transfers between devices: 112 us -> none  [gather_hidden(): return lax.all_gather(stacked, 'row', axis=1, tiled=True)]
    ppermute x0 -> x30, starting transfers between devices: none -> 70.8 us  [the longest x14 68.8 us: divide_the_slots(): lax.ppermute(far_arr, axis_name=across, perm=list(map(lambda no: (no, (no...]
    ppermute x0 -> x30, waiting for transfers between devices: none -> 68.2 us  [the longest x16 37.4 us: divide_the_slots(): view_out = lax.ppermute(view_out, axis_name=across, perm=list(arr_out))]
    dynamic_update_slice x0 -> x30, local copies, waits for them, and re-layouts: none -> 22.7 us  [the longest x16 12.1 us: divide_the_slots(): lax.dynamic_update_slice_in_dim(val2, view_out, (w_next - j0) % a_next *...]
  transfers between devices with their start and end apart: 9 -> 37, of which waited for: 8 -> 26; matrix products, arithmetic and copies ran while one was open for 7% -> 11% of each run, Pallas kernels for 0% -> 0%
where the time goes in v1:
time: 545 us; the launch traced here: 544 us
  waiting for transfers between devices  302 us (55%)
  starting transfers between devices  71.1 us (13%)
  blocking collectives  57.1 us (10%)
  matrix products  47.5 us (9%)
  local copies, waits for them, and re-layouts  36.1 us (7%)
  other arithmetic  15.5 us (3%)
  between operations  14.3 us (3%)
    reduce_scatter x1, waiting for transfers between devices, per_device(): lax.psum_scatter(jnp.concatenate([jnp.dot(rows, gate_weight, preferred_el...  84.9 us
    reduce_scatter x1, waiting for transfers between devices, per_device(): lax.psum_scatter(right_transpose(rows, down_weight).astype(jnp.bfloat16),...  81 us
    ppermute x14, starting transfers between devices, divide_the_slots(): lax.ppermute(far_arr, axis_name=across, perm=list(map(lambda no: (no, (no...  68.8 us
    ppermute x16, waiting for transfers between devices, divide_the_slots(): view_out = lax.ppermute(view_out, axis_name=across, perm=list(arr_out))  37.4 us
    reduce_scatter x2, waiting for transfers between devices, column_total(): lax.psum_scatter(term_fn(jnp.int32(0), count_rows * lax.axis_size('col'))...  36.4 us
    psum x1, blocking collectives, per_device(): score = lax.psum(partial_score, 'row')  33.1 us
    ppermute x14, waiting for transfers between devices, divide_the_slots(): lax.ppermute(far_arr, axis_name=across, perm=list(map(lambda no: (no, (no...  30.9 us
    all_gather x2, blocking collectives, gather_tokens(): return lax.all_gather(block, 'col', axis=0, tiled=True)  24 us
  transfers between devices with their start and end apart: 37, of which 26 were waited for; matrix products, arithmetic and copies ran while one was open for 11% of the time, Pallas kernels for 0%

profile of v1, /device:TPU:1, one launch (start us, length us, event | category | flops | bytes accessed | tf_op | source)
XLA Modules:
  0.0 544.0 jit_solution(7773975374798200609)
XLA Ops:
  7.2 13.6 %all_gather.6 = bf16[512,512]{1,0:T(8,128)(2,1)S(1)} all-gather(bf16[128,512]{1,0:T(8,128)(2,1)} %param.8), channel_id=1, replica_groups=mesh['row'=16,'col'=4,'dp'=2] {'col'}, dimensions={0}, use_global_device_ids=true | all-gather | bytes 655360 | tf_op jit(solution)/shard_map/all_gather | solution.py:50
  20.8 4.3 convolution_convert_fusion.4
  25.1 3.9 convolution_convert_fusion.5
  29.0 5.9 %pad_maximum_fusion = bf16[512,7168]{1,0:T(8,128)(2,1)} fusion(bf16[512,3584]{1,0:T(8,128)(2,1)S(1)} %convolution_convert_fusion.4, bf16[512,3584]{1,0:T(8,128)(2,1)} %convolution_convert_fusion.5), kind=kLoop, calls=%fused_computation | loop fusion | flops 14680064 | bytes 14680064 | tf_op jit(solution)/shard_map/concatenate | solution.py:73
  35.0 84.9 %reduce-scatter.8.cloned.1.call-done = bf16[32,7168]{1,0:T(8,128)(2,1)} async-done(((bf16[512,7168]{1,0:T(8,128)(2,1)}), bf16[32,7168]{1,0:T(8,128)(2,1)}) %reduce-scatter.8.cloned.1.call-update) | async-done | bytes 458768 | tf_op jit(solution)/shard_map/reduce_scatter | solution.py:72
  120.0 1.1 convert_element_type.76
  121.1 2.1 squeeze.41
  123.9 0.9 collective-permute-start
  124.9 3.9 collective-permute-start.1
  128.7 3.7 collective-permute-done
  132.5 4.8 collective-permute-start.3
  138.7 2.0 collective-permute-done.2
  140.7 4.8 collective-permute-start.5
  146.8 2.0 collective-permute-done.4
  148.8 4.8 collective-permute-start.7
  155.0 2.0 collective-permute-done.6
  157.0 4.8 collective-permute-start.9
  163.2 2.0 collective-permute-done.8
  165.2 4.9 collective-permute-start.11
  171.6 2.9 collective-permute-done.10
  174.4 5.1 collective-permute-start.13
  181.0 3.8 collective-permute-done.12
  186.1 8.7 %collective-permute-done.14 = bf16[1,32,3584]{2,1,0:T(8,128)(2,1)S(1)} collective-permute-done((bf16[1,32,3584]{2,1,0:T(8,128)(2,1)S(1)}, bf16[1,32,3584]{2,1,0:T(8,128)(2,1)S(1)}, u32[]{:S(2)}, u32[]{:S(2)}) %collective-permute-start.14) | collective-permute-done | bytes 229408 | tf_op jit(solution)/shard_map/ppermute | solution.py:21
  195.6 5.0 convolution_convert_fusion.6
  200.7 26.2 %reduce-scatter.10.cloned.1.call-done = bf16[128,512]{1,0:T(8,128)(2,1)} async-done(((bf16[512,512]{1,0:T(8,128)(2,1)}), bf16[128,512]{1,0:T(8,128)(2,1)}) %reduce-scatter.10.cloned.1.call-update) | async-done | bytes 131088 | tf_op jit(solution)/shard_map/reduce_scatter | solution.py:58
  226.9 1.1 convolution_bitcast_fusion
  228.0 33.1 %psum.7 = f32[128]{0:T(128)S(1)} all-reduce(f32[128]{0:T(128)S(1)} %convolution_bitcast_fusion), channel_id=1, replica_groups=mesh['row'=16,'col'=4,'dp'=2] {'row'}, use_global_device_ids=true, to_apply=%region_2.3 | all-reduce | flops 128 | bytes 1024 | tf_op jit(solution)/shard_map/psum | solution.py:97
  261.3 10.4 %all_gather.7 = bf16[512,512]{1,0:T(8,128)(2,1)S(1)} all-gather(bf16[128,512]{1,0:T(8,128)(2,1)S(1)} %fusion.14), channel_id=1, replica_groups=mesh['row'=16,'col'=4,'dp'=2] {'col'}, dimensions={0}, use_global_device_ids=true | all-gather | bytes 655360 | tf_op jit(solution)/shard_map/all_gather | solution.py:50
  271.7 6.0 %convolution_convert_fusion.3 = bf16[512,3584]{1,0:T(8,128)(2,1)} fusion(bf16[512,512]{1,0:T(8,128)(2,1)S(1)} %all_gather.7, bf16[3584,512]{1,0:T(8,128)(2,1)} %param.11), kind=kOutput, calls=%fused_computation.4 | convolution fusion | flops 1880883200 | bytes 7864320 | tf_op jit(solution)/shard_map/dot_general | solution.py:44
  277.7 81.0 %reduce-scatter.12.cloned.1.call-done = bf16[32,3584]{1,0:T(8,128)(2,1)} async-done(((bf16[512,3584]{1,0:T(8,128)(2,1)}), bf16[32,3584]{1,0:T(8,128)(2,1)}) %reduce-scatter.12.cloned.1.call-update) | async-done | bytes 229392 | tf_op jit(solution)/shard_map/reduce_scatter | solution.py:107
  358.7 1.2 fusion.16
  359.9 3.4 broadcast_in_dim.4
  363.3 0.8 pad_maximum_fusion.1
  364.1 1.0 collective-permute-start.15
  365.1 6.1 %convolution_convert_fusion = bf16[3584,512]{1,0:T(8,128)(2,1)} fusion(bf16[512,3584]{1,0:T(8,128)(2,1)} %bitcast_dynamic-update-slice_fusion, bf16[512,512]{1,0:T(8,128)(2,1)S(1)} %all_gather.7), kind=kOutput, calls=%fused_computation.1 | convolution fusion | flops 1880883200 | bytes 7864320 | tf_op jit(solution)/shard_map/dot_general | solution.py:38
  371.2 3.9 collective-permute-start.16
  375.1 2.0 collective-permute-done.15
  377.9 4.4 collective-permute-done.16
  382.3 5.5 %collective-permute-start.18 = (bf16[2,32,3584]{2,1,0:T(8,128)(2,1)S(1)}, bf16[2,32,3584]{2,1,0:T(8,128)(2,1)S(1)}, u32[]{:S(2)}, u32[]{:S(2)}) collective-permute-start(bf16[2,32,3584]{2,1,0:T(8,128)(2,1)S(1)} %collective-permute-done.16), channel_id=1, source_target_pairs={{0,120},{8,0},{16,8},{24,16},{32,24},{40,32},{48,40},{56,48},{64,5... | collective-permute-start | bytes 1376264 | tf_op jit(solution)/shard_map/ppermute | solution.py:26
  389.1 4.9 collective-permute-done.18
  394.0 5.5 %collective-permute-start.20 = (bf16[2,32,3584]{2,1,0:T(8,128)(2,1)S(1)}, bf16[2,32,3584]{2,1,0:T(8,128)(2,1)S(1)}, u32[]{:S(2)}, u32[]{:S(2)}) collective-permute-start(bf16[2,32,3584]{2,1,0:T(8,128)(2,1)S(1)} %collective-permute-done.18), channel_id=1, source_target_pairs={{0,120},{8,0},{16,8},{24,16},{32,24},{40,32},{48,40},{56,48},{64,5... | collective-permute-start | bytes 1376264 | tf_op jit(solution)/shard_map/ppermute | solution.py:26
  401.2 3.8 collective-permute-done.20
  405.0 5.2 collective-permute-start.22
  410.2 0.8 constant_dynamic-update-slice_fusion.10
  411.9 3.8 collective-permute-done.22
  415.6 5.2 collective-permute-start.24
  421.7 0.8 constant_dynamic-update-slice_fusion.7
  422.5 4.1 collective-permute-done.24
  426.6 5.2 collective-permute-start.26
  433.8 4.9 collective-permute-done.26
  438.7 5.2 collective-permute-start.28
  447.0 4.9 collective-permute-done.28
  452.7 6.9 %collective-permute-done.29 = bf16[2,32,3584]{2,1,0:T(8,128)(2,1)S(1)} collective-permute-done((bf16[2,32,3584]{2,1,0:T(8,128)(2,1)S(1)}, bf16[2,32,3584]{2,1,0:T(8,128)(2,1)S(1)}, u32[]{:S(2)}, u32[]{:S(2)}) %collective-permute-start.29) | collective-permute-done | bytes 458784 | tf_op jit(solution)/shard_map/ppermute | solution.py:21
  460.4 4.3 fusion.3
  464.7 4.9 fusion.5
  469.7 6.0 %fusion.1 = bf16[512,3584]{0,1:T(8,128)(2,1)} fusion(bf16[512,512]{1,0:T(8,128)(2,1)S(1)} %all_gather.6, bf16[2,512,3584]{2,1,0:T(8,128)(2,1)} %constant_dynamic-update-slice_fusion), kind=kOutput, calls=%fused_computation.8 | convolution fusion | flops 1880883200 | bytes 7864320 | tf_op jit(solution)/shard_map/dot_general | solution.py:38
  475.8 6.0 %fusion = bf16[512,3584]{0,1:T(8,128)(2,1)} fusion(bf16[512,512]{1,0:T(8,128)(2,1)S(1)} %all_gather.6, bf16[2,512,3584]{2,1,0:T(8,128)(2,1)} %constant_dynamic-update-slice_fusion), kind=kOutput, calls=%fused_computation.7 | convolution fusion | flops 1880883200 | bytes 7864320 | tf_op jit(solution)/shard_map/dot_general | solution.py:38
  481.8 3.9 convert_element_type.94
  485.7 10.1 %reduce-scatter.20.cloned.1.call-done = bf16[128,512]{1,0:T(8,128)(2,1)} async-done(((bf16[512,512]{1,0:T(8,128)(2,1)}), bf16[128,512]{1,0:T(8,128)(2,1)}) %reduce-scatter.20.cloned.1.call-update) | async-done | bytes 131088 | tf_op jit(solution)/shard_map/reduce_scatter | solution.py:58
  495.8 1.7 convert_add_fusion
  497.5 17.0 %reduce-scatter.16.cloned.1.call-done = bf16[256,3584]{0,1:T(8,128)(2,1)} async-done(((bf16[512,3584]{0,1:T(8,128)(2,1)}), bf16[256,3584]{0,1:T(8,128)(2,1)}) %reduce-scatter.16.cloned.1.call-update) | async-done | bytes 1835024 | tf_op jit(solution)/shard_map/reduce_scatter | solution.py:130
  514.5 4.0 copy.13
  518.5 14.7 %reduce-scatter.14.cloned.1.call-done = bf16[256,3584]{0,1:T(8,128)(2,1)} async-done(((bf16[512,3584]{0,1:T(8,128)(2,1)}), bf16[256,3584]{0,1:T(8,128)(2,1)}) %reduce-scatter.14.cloned.1.call-update) | async-done | bytes 1835024 | tf_op jit(solution)/shard_map/reduce_scatter | solution.py:124
  533.2 4.0 copy.12
  (93 shorter events, 23.9 us)
Async XLA Ops:
  7.2 112.8 %reduce-scatter.8.cloned.1.call-start = ((), (), s32[]{:S(2)}) async-start(), calls=%async_computation.7 | async-start | bytes 7798784 | tf_op jit(solution)/shard_map/reduce_scatter | solution.py:72
  20.8 4.3 copy-start.7
  35.0 191.9 %reduce-scatter.10.cloned.1.call-start = ((), (), s32[]{:S(2)}) async-start(), calls=%async_computation.8 | async-start | bytes 655360 | tf_op jit(solution)/shard_map/reduce_scatter | solution.py:58
  123.9 8.5 %collective-permute-start = (bf16[1,32,3584]{2,1,0:T(8,128)(2,1)S(1)}, bf16[1,32,3584]{2,1,0:T(8,128)(2,1)S(1)}, u32[]{:S(2)}, u32[]{:S(2)}) collective-permute-start(bf16[1,32,3584]{2,1,0:T(8,128)(2,1)S(1)} %bitcast.68), channel_id=1, source_target_pairs={{0,8},{8,16},{16,24},{24,32},{32,40},{40,48},{48,56},{56,64},{64,7... | collective-permute-start | bytes 688136 | tf_op jit(solution)/shard_map/ppermute | solution.py:21
  124.9 7.6 %collective-permute-start.1 = (bf16[1,32,3584]{2,1,0:T(8,128)(2,1)S(1)}, bf16[1,32,3584]{2,1,0:T(8,128)(2,1)S(1)}, u32[]{:S(2)}, u32[]{:S(2)}) collective-permute-start(bf16[1,32,3584]{2,1,0:T(8,128)(2,1)S(1)} %bitcast.69), channel_id=1, source_target_pairs={{0,120},{8,0},{16,8},{24,16},{32,24},{40,32},{48,40},{56,48},{64,5... | collective-permute-start | bytes 688136 | tf_op jit(solution)/shard_map/ppermute | solution.py:26
  128.7 66.8 %copy-start.5 = (bf16[3584,512]{1,0:T(8,128)(2,1)S(1)}, bf16[3584,512]{1,0:T(8,128)(2,1)}, u32[]{:S(2)}) copy-start(bf16[3584,512]{1,0:T(8,128)(2,1)} %param.11) | copy-start | bytes 11010052
  132.5 8.2 %collective-permute-start.2 = (bf16[1,32,3584]{2,1,0:T(8,128)(2,1)S(1)}, bf16[1,32,3584]{2,1,0:T(8,128)(2,1)S(1)}, u32[]{:S(2)}, u32[]{:S(2)}) collective-permute-start(bf16[1,32,3584]{2,1,0:T(8,128)(2,1)S(1)} %collective-permute-done), channel_id=1, source_target_pairs={{0,8},{8,16},{16,24},{24,32},{32,40},{40,48},{48,56},{56,64},{64,7... | collective-permute-start | bytes 688136 | tf_op jit(solution)/shard_map/ppermute | solution.py:21
  132.5 8.2 %collective-permute-start.3 = (bf16[1,32,3584]{2,1,0:T(8,128)(2,1)S(1)}, bf16[1,32,3584]{2,1,0:T(8,128)(2,1)S(1)}, u32[]{:S(2)}, u32[]{:S(2)}) collective-permute-start(bf16[1,32,3584]{2,1,0:T(8,128)(2,1)S(1)} %collective-permute-done.1), channel_id=1, source_target_pairs={{0,120},{8,0},{16,8},{24,16},{32,24},{40,32},{48,40},{56,48},{64,5... | collective-permute-start | bytes 688136 | tf_op jit(solution)/shard_map/ppermute | solution.py:26
  140.6 8.2 %collective-permute-start.4 = (bf16[1,32,3584]{2,1,0:T(8,128)(2,1)S(1)}, bf16[1,32,3584]{2,1,0:T(8,128)(2,1)S(1)}, u32[]{:S(2)}, u32[]{:S(2)}) collective-permute-start(bf16[1,32,3584]{2,1,0:T(8,128)(2,1)S(1)} %collective-permute-done.2), channel_id=1, source_target_pairs={{0,8},{8,16},{16,24},{24,32},{32,40},{40,48},{48,56},{56,64},{64,7... | collective-permute-start | bytes 688136 | tf_op jit(solution)/shard_map/ppermute | solution.py:21
  140.7 8.2 %collective-permute-start.5 = (bf16[1,32,3584]{2,1,0:T(8,128)(2,1)S(1)}, bf16[1,32,3584]{2,1,0:T(8,128)(2,1)S(1)}, u32[]{:S(2)}, u32[]{:S(2)}) collective-permute-start(bf16[1,32,3584]{2,1,0:T(8,128)(2,1)S(1)} %collective-permute-done.3), channel_id=1, source_target_pairs={{0,120},{8,0},{16,8},{24,16},{32,24},{40,32},{48,40},{56,48},{64,5... | collective-permute-start | bytes 688136 | tf_op jit(solution)/shard_map/ppermute | solution.py:26
  148.8 8.2 %collective-permute-start.6 = (bf16[1,32,3584]{2,1,0:T(8,128)(2,1)S(1)}, bf16[1,32,3584]{2,1,0:T(8,128)(2,1)S(1)}, u32[]{:S(2)}, u32[]{:S(2)}) collective-permute-start(bf16[1,32,3584]{2,1,0:T(8,128)(2,1)S(1)} %collective-permute-done.4), channel_id=1, source_target_pairs={{0,8},{8,16},{16,24},{24,32},{32,40},{40,48},{48,56},{56,64},{64,7... | collective-permute-start | bytes 688136 | tf_op jit(solution)/shard_map/ppermute | solution.py:21
  148.8 8.2 %collective-permute-start.7 = (bf16[1,32,3584]{2,1,0:T(8,128)(2,1)S(1)}, bf16[1,32,3584]{2,1,0:T(8,128)(2,1)S(1)}, u32[]{:S(2)}, u32[]{:S(2)}) collective-permute-start(bf16[1,32,3584]{2,1,0:T(8,128)(2,1)S(1)} %collective-permute-done.5), channel_id=1, source_target_pairs={{0,120},{8,0},{16,8},{24,16},{32,24},{40,32},{48,40},{56,48},{64,5... | collective-permute-start | bytes 688136 | tf_op jit(solution)/shard_map/ppermute | solution.py:26
  157.0 8.2 %collective-permute-start.8 = (bf16[1,32,3584]{2,1,0:T(8,128)(2,1)S(1)}, bf16[1,32,3584]{2,1,0:T(8,128)(2,1)S(1)}, u32[]{:S(2)}, u32[]{:S(2)}) collective-permute-start(bf16[1,32,3584]{2,1,0:T(8,128)(2,1)S(1)} %collective-permute-done.6), channel_id=1, source_target_pairs={{0,8},{8,16},{16,24},{24,32},{32,40},{40,48},{48,56},{56,64},{64,7... | collective-permute-start | bytes 688136 | tf_op jit(solution)/shard_map/ppermute | solution.py:21
  157.0 8.2 %collective-permute-start.9 = (bf16[1,32,3584]{2,1,0:T(8,128)(2,1)S(1)}, bf16[1,32,3584]{2,1,0:T(8,128)(2,1)S(1)}, u32[]{:S(2)}, u32[]{:S(2)}) collective-permute-start(bf16[1,32,3584]{2,1,0:T(8,128)(2,1)S(1)} %collective-permute-done.7), channel_id=1, source_target_pairs={{0,120},{8,0},{16,8},{24,16},{32,24},{40,32},{48,40},{56,48},{64,5... | collective-permute-start | bytes 688136 | tf_op jit(solution)/shard_map/ppermute | solution.py:26
  165.2 9.2 %collective-permute-start.10 = (bf16[1,32,3584]{2,1,0:T(8,128)(2,1)S(1)}, bf16[1,32,3584]{2,1,0:T(8,128)(2,1)S(1)}, u32[]{:S(2)}, u32[]{:S(2)}) collective-permute-start(bf16[1,32,3584]{2,1,0:T(8,128)(2,1)S(1)} %collective-permute-done.8), channel_id=1, source_target_pairs={{0,8},{8,16},{16,24},{24,32},{32,40},{40,48},{48,56},{56,64},{64,7... | collective-permute-start | bytes 688136 | tf_op jit(solution)/shard_map/ppermute | solution.py:21
  165.2 9.2 %collective-permute-start.11 = (bf16[1,32,3584]{2,1,0:T(8,128)(2,1)S(1)}, bf16[1,32,3584]{2,1,0:T(8,128)(2,1)S(1)}, u32[]{:S(2)}, u32[]{:S(2)}) collective-permute-start(bf16[1,32,3584]{2,1,0:T(8,128)(2,1)S(1)} %collective-permute-done.9), channel_id=1, source_target_pairs={{0,120},{8,0},{16,8},{24,16},{32,24},{40,32},{48,40},{56,48},{64,5... | collective-permute-start | bytes 688136 | tf_op jit(solution)/shard_map/ppermute | solution.py:26
  174.4 10.3 %collective-permute-start.12 = (bf16[1,32,3584]{2,1,0:T(8,128)(2,1)S(1)}, bf16[1,32,3584]{2,1,0:T(8,128)(2,1)S(1)}, u32[]{:S(2)}, u32[]{:S(2)}) collective-permute-start(bf16[1,32,3584]{2,1,0:T(8,128)(2,1)S(1)} %collective-permute-done.10), channel_id=1, source_target_pairs={{0,8},{8,16},{16,24},{24,32},{32,40},{40,48},{48,56},{56,64},{64,7... | collective-permute-start | bytes 688136 | tf_op jit(solution)/shard_map/ppermute | solution.py:21
  174.4 11.0 %collective-permute-start.13 = (bf16[1,32,3584]{2,1,0:T(8,128)(2,1)S(1)}, bf16[1,32,3584]{2,1,0:T(8,128)(2,1)S(1)}, u32[]{:S(2)}, u32[]{:S(2)}) collective-permute-start(bf16[1,32,3584]{2,1,0:T(8,128)(2,1)S(1)} %collective-permute-done.11), channel_id=1, source_target_pairs={{0,120},{8,0},{16,8},{24,16},{32,24},{40,32},{48,40},{56,48},{64,5... | collective-permute-start | bytes 688136 | tf_op jit(solution)/shard_map/ppermute | solution.py:26
  184.7 10.1 %collective-permute-start.14 = (bf16[1,32,3584]{2,1,0:T(8,128)(2,1)S(1)}, bf16[1,32,3584]{2,1,0:T(8,128)(2,1)S(1)}, u32[]{:S(2)}, u32[]{:S(2)}) collective-permute-start(bf16[1,32,3584]{2,1,0:T(8,128)(2,1)S(1)} %collective-permute-done.12), channel_id=1, source_target_pairs={{0,8},{8,16},{16,24},{24,32},{32,40},{40,48},{48,56},{56,64},{64,7... | collective-permute-start | bytes 688136 | tf_op jit(solution)/shard_map/ppermute | solution.py:21
  195.5 5.1 copy-start.2
  195.5 31.4 %copy-start = (bf16[128,512]{1,0:T(8,128)(2,1)S(1)}, bf16[128,512]{1,0:T(8,128)(2,1)}, u32[]{:S(2)}) copy-start(bf16[128,512]{1,0:T(8,128)(2,1)} %param.8) | copy-start | bytes 393220
  195.5 65.6 %copy-start.3 = (s32[128]{0:T(128)S(1)}, s32[128]{0:T(128)}, u32[]{:S(2)}) copy-start(s32[128]{0:T(128)} %param.14) | copy-start | bytes 1540
  195.6 65.6 %copy-start.4 = (s32[128]{0:T(128)S(1)}, s32[128]{0:T(128)}, u32[]{:S(2)}) copy-start(s32[128]{0:T(128)} %param.15) | copy-start | bytes 1540
  195.6 65.6 %copy-start.1 = (bf16[128,512]{1,0:T(8,128)(2,1)S(1)}, bf16[128,512]{1,0:T(8,128)(2,1)}, u32[]{:S(2)}) copy-start(bf16[128,512]{1,0:T(8,128)(2,1)} %param.13) | copy-start | bytes 393220
  200.6 158.2 %reduce-scatter.12.cloned.1.call-start = ((), (), s32[]{:S(2)}) async-start(), calls=%async_computation.9 | async-start | bytes 3899392 | tf_op jit(solution)/shard_map/reduce_scatter | solution.py:107
  277.7 204.2 %reduce-scatter.18.cloned.1.call-start = ((), (), s32[]{:S(2)}) async-start(), calls=%async_computation.12 | async-start | bytes 5505024 | tf_op jit(solution)/shard_map/reduce_scatter | solution.py:136
  364.1 13.0 %collective-permute-start.15 = (bf16[2,32,3584]{2,1,0:T(8,128)(2,1)S(1)}, bf16[2,32,3584]{2,1,0:T(8,128)(2,1)S(1)}, u32[]{:S(2)}, u32[]{:S(2)}) collective-permute-start(bf16[2,32,3584]{2,1,0:T(8,128)(2,1)S(1)} %get-tuple-element.12), channel_id=1, source_target_pairs={{0,8},{8,16},{16,24},{24,32},{32,40},{40,48},{48,56},{56,64},{64,7... | collective-permute-start | bytes 1376264 | tf_op jit(solution)/shard_map/ppermute | solution.py:21
  371.2 124.6 %reduce-scatter.20.cloned.1.call-start = ((), (), s32[]{:S(2)}) async-start(), calls=%async_computation.13 | async-start | bytes 655360 | tf_op jit(solution)/shard_map/reduce_scatter | solution.py:58
  371.2 11.0 %collective-permute-start.16 = (bf16[2,32,3584]{2,1,0:T(8,128)(2,1)S(1)}, bf16[2,32,3584]{2,1,0:T(8,128)(2,1)S(1)}, u32[]{:S(2)}, u32[]{:S(2)}) collective-permute-start(bf16[2,32,3584]{2,1,0:T(8,128)(2,1)S(1)} %get-tuple-element.12), channel_id=1, source_target_pairs={{0,120},{8,0},{16,8},{24,16},{32,24},{40,32},{48,40},{56,48},{64,5... | collective-permute-start | bytes 1376264 | tf_op jit(solution)/shard_map/ppermute | solution.py:26
  377.1 12.0 %collective-permute-start.17 = (bf16[2,32,3584]{2,1,0:T(8,128)(2,1)S(1)}, bf16[2,32,3584]{2,1,0:T(8,128)(2,1)S(1)}, u32[]{:S(2)}, u32[]{:S(2)}) collective-permute-start(bf16[2,32,3584]{2,1,0:T(8,128)(2,1)S(1)} %collective-permute-done.15), channel_id=1, source_target_pairs={{0,8},{8,16},{16,24},{24,32},{32,40},{40,48},{48,56},{56,64},{64,7... | collective-permute-start | bytes 1376264 | tf_op jit(solution)/shard_map/ppermute | solution.py:21
  382.3 11.8 %collective-permute-start.18 = (bf16[2,32,3584]{2,1,0:T(8,128)(2,1)S(1)}, bf16[2,32,3584]{2,1,0:T(8,128)(2,1)S(1)}, u32[]{:S(2)}, u32[]{:S(2)}) collective-permute-start(bf16[2,32,3584]{2,1,0:T(8,128)(2,1)S(1)} %collective-permute-done.16), channel_id=1, source_target_pairs={{0,120},{8,0},{16,8},{24,16},{32,24},{40,32},{48,40},{56,48},{64,5... | collective-permute-start | bytes 1376264 | tf_op jit(solution)/shard_map/ppermute | solution.py:26
  389.1 12.0 %collective-permute-start.19 = (bf16[2,32,3584]{2,1,0:T(8,128)(2,1)S(1)}, bf16[2,32,3584]{2,1,0:T(8,128)(2,1)S(1)}, u32[]{:S(2)}, u32[]{:S(2)}) collective-permute-start(bf16[2,32,3584]{2,1,0:T(8,128)(2,1)S(1)} %collective-permute-done.17), channel_id=1, source_target_pairs={{0,8},{8,16},{16,24},{24,32},{32,40},{40,48},{48,56},{56,64},{64,7... | collective-permute-start | bytes 1376264 | tf_op jit(solution)/shard_map/ppermute | solution.py:21
  394.0 10.9 %collective-permute-start.20 = (bf16[2,32,3584]{2,1,0:T(8,128)(2,1)S(1)}, bf16[2,32,3584]{2,1,0:T(8,128)(2,1)S(1)}, u32[]{:S(2)}, u32[]{:S(2)}) collective-permute-start(bf16[2,32,3584]{2,1,0:T(8,128)(2,1)S(1)} %collective-permute-done.18), channel_id=1, source_target_pairs={{0,120},{8,0},{16,8},{24,16},{32,24},{40,32},{48,40},{56,48},{64,5... | collective-permute-start | bytes 1376264 | tf_op jit(solution)/shard_map/ppermute | solution.py:26
  401.1 10.7 %collective-permute-start.21 = (bf16[2,32,3584]{2,1,0:T(8,128)(2,1)S(1)}, bf16[2,32,3584]{2,1,0:T(8,128)(2,1)S(1)}, u32[]{:S(2)}, u32[]{:S(2)}) collective-permute-start(bf16[2,32,3584]{2,1,0:T(8,128)(2,1)S(1)} %collective-permute-done.19), channel_id=1, source_target_pairs={{0,8},{8,16},{16,24},{24,32},{32,40},{40,48},{48,56},{56,64},{64,7... | collective-permute-start | bytes 1376264 | tf_op jit(solution)/shard_map/ppermute | solution.py:21
  405.0 10.6 %collective-permute-start.22 = (bf16[2,32,3584]{2,1,0:T(8,128)(2,1)S(1)}, bf16[2,32,3584]{2,1,0:T(8,128)(2,1)S(1)}, u32[]{:S(2)}, u32[]{:S(2)}) collective-permute-start(bf16[2,32,3584]{2,1,0:T(8,128)(2,1)S(1)} %collective-permute-done.20), channel_id=1, source_target_pairs={{0,120},{8,0},{16,8},{24,16},{32,24},{40,32},{48,40},{56,48},{64,5... | collective-permute-start | bytes 1376264 | tf_op jit(solution)/shard_map/ppermute | solution.py:26
  411.9 10.7 %collective-permute-start.23 = (bf16[2,32,3584]{2,1,0:T(8,128)(2,1)S(1)}, bf16[2,32,3584]{2,1,0:T(8,128)(2,1)S(1)}, u32[]{:S(2)}, u32[]{:S(2)}) collective-permute-start(bf16[2,32,3584]{2,1,0:T(8,128)(2,1)S(1)} %collective-permute-done.21), channel_id=1, source_target_pairs={{0,8},{8,16},{16,24},{24,32},{32,40},{40,48},{48,56},{56,64},{64,7... | collective-permute-start | bytes 1376264 | tf_op jit(solution)/shard_map/ppermute | solution.py:21
  415.6 11.0 %collective-permute-start.24 = (bf16[2,32,3584]{2,1,0:T(8,128)(2,1)S(1)}, bf16[2,32,3584]{2,1,0:T(8,128)(2,1)S(1)}, u32[]{:S(2)}, u32[]{:S(2)}) collective-permute-start(bf16[2,32,3584]{2,1,0:T(8,128)(2,1)S(1)} %collective-permute-done.22), channel_id=1, source_target_pairs={{0,120},{8,0},{16,8},{24,16},{32,24},{40,32},{48,40},{56,48},{64,5... | collective-permute-start | bytes 1376264 | tf_op jit(solution)/shard_map/ppermute | solution.py:26
  421.7 38.8 %copy-start.6 = (bf16[512,3584]{1,0:T(8,128)(2,1)S(1)}, bf16[512,3584]{1,0:T(8,128)(2,1)}, u32[]{:S(2)}) copy-start(bf16[512,3584]{1,0:T(8,128)(2,1)} %param.10) | copy-start | bytes 11010052
  422.5 11.3 %collective-permute-start.25 = (bf16[2,32,3584]{2,1,0:T(8,128)(2,1)S(1)}, bf16[2,32,3584]{2,1,0:T(8,128)(2,1)S(1)}, u32[]{:S(2)}, u32[]{:S(2)}) collective-permute-start(bf16[2,32,3584]{2,1,0:T(8,128)(2,1)S(1)} %collective-permute-done.23), channel_id=1, source_target_pairs={{0,8},{8,16},{16,24},{24,32},{32,40},{40,48},{48,56},{56,64},{64,7... | collective-permute-start | bytes 1376264 | tf_op jit(solution)/shard_map/ppermute | solution.py:21
  426.6 12.1 %collective-permute-start.26 = (bf16[2,32,3584]{2,1,0:T(8,128)(2,1)S(1)}, bf16[2,32,3584]{2,1,0:T(8,128)(2,1)S(1)}, u32[]{:S(2)}, u32[]{:S(2)}) collective-permute-start(bf16[2,32,3584]{2,1,0:T(8,128)(2,1)S(1)} %collective-permute-done.24), channel_id=1, source_target_pairs={{0,120},{8,0},{16,8},{24,16},{32,24},{40,32},{48,40},{56,48},{64,5... | collective-permute-start | bytes 1376264 | tf_op jit(solution)/shard_map/ppermute | solution.py:26
  433.8 12.4 %collective-permute-start.27 = (bf16[2,32,3584]{2,1,0:T(8,128)(2,1)S(1)}, bf16[2,32,3584]{2,1,0:T(8,128)(2,1)S(1)}, u32[]{:S(2)}, u32[]{:S(2)}) collective-permute-start(bf16[2,32,3584]{2,1,0:T(8,128)(2,1)S(1)} %collective-permute-done.25), channel_id=1, source_target_pairs={{0,8},{8,16},{16,24},{24,32},{32,40},{40,48},{48,56},{56,64},{64,7... | collective-permute-start | bytes 1376264 | tf_op jit(solution)/shard_map/ppermute | solution.py:21
  438.7 13.2 %collective-permute-start.28 = (bf16[2,32,3584]{2,1,0:T(8,128)(2,1)S(1)}, bf16[2,32,3584]{2,1,0:T(8,128)(2,1)S(1)}, u32[]{:S(2)}, u32[]{:S(2)}) collective-permute-start(bf16[2,32,3584]{2,1,0:T(8,128)(2,1)S(1)} %collective-permute-done.26), channel_id=1, source_target_pairs={{0,120},{8,0},{16,8},{24,16},{32,24},{40,32},{48,40},{56,48},{64,5... | collective-permute-start | bytes 1376264 | tf_op jit(solution)/shard_map/ppermute | solution.py:26
  446.2 13.5 %collective-permute-start.29 = (bf16[2,32,3584]{2,1,0:T(8,128)(2,1)S(1)}, bf16[2,32,3584]{2,1,0:T(8,128)(2,1)S(1)}, u32[]{:S(2)}, u32[]{:S(2)}) collective-permute-start(bf16[2,32,3584]{2,1,0:T(8,128)(2,1)S(1)} %collective-permute-done.27), channel_id=1, source_target_pairs={{0,8},{8,16},{16,24},{24,32},{32,40},{40,48},{48,56},{56,64},{64,7... | collective-permute-start | bytes 1376264 | tf_op jit(solution)/shard_map/ppermute | solution.py:21
  460.4 4.3 copy-start.8
  469.7 44.9 %reduce-scatter.16.cloned.1.call-start = ((), (), s32[]{:S(2)}) async-start(), calls=%async_computation.11 | async-start | bytes 5505024 | tf_op jit(solution)/shard_map/reduce_scatter | solution.py:130
  475.7 57.5 %reduce-scatter.14.cloned.1.call-start = ((), (), s32[]{:S(2)}) async-start(), calls=%async_computation.10 | async-start | bytes 5505024 | tf_op jit(solution)/shard_map/reduce_scatter | solution.py:124
Sparse Core Ops, SparseCore 0:
  35.1 84.8 reduce-scatter.7
  200.7 26.1 reduce-scatter.9
  277.8 80.9 reduce-scatter.11
  371.3 17.1 reduce-scatter.17
  469.8 25.9 reduce-scatter.19
  498.6 15.8 reduce-scatter.15
  517.6 15.5 reduce-scatter.13
